TPU v7x, 128 devices: a whole 4x4x4 slice. The times are simulated.
128 devices in a mesh: req: 32 (over z, y, core), tp: 4 (over x).
Axes of the slice: x: 4, y: 4, z: 4, core: 2. Of those that a mesh axis runs over, the one named last changes fastest.
Arguments:
- tokens: bfloat16 [16384, 2048], P('req', 'tp')
- lengths: int32 [32, 16], P('req'), may hold values from 1 to 36, 512 in all within a row
- request_adapter_index: int32 [32, 16], P('req'), may hold values from 0 to 63, as said below
- attention_norm_gain: float32 [2048], replicated, may hold values from 0.5 to 1.5
- query_norm_gain: float32 [128], replicated, may hold values from 0.5 to 1.5
- key_norm_gain: float32 [128], replicated, may hold values from 0.5 to 1.5
- feedforward_norm_gain: float32 [2048], replicated, may hold values from 0.5 to 1.5
- query_weight: bfloat16 [2048, 2048], P(None, 'tp'), may hold values from -0.125 to 0.125
- key_weight: bfloat16 [2048, 1024], P(None, 'tp'), may hold values from -0.125 to 0.125
- value_weight: bfloat16 [2048, 1024], P(None, 'tp'), may hold values from -0.125 to 0.125
- output_weight: bfloat16 [2048, 2048], P('tp'), may hold values from -0.125 to 0.125
- gate_weight: bfloat16 [2048, 3072], P(None, 'tp'), may hold values from -0.125 to 0.125
- up_weight: bfloat16 [2048, 3072], P(None, 'tp'), may hold values from -0.125 to 0.125
- down_weight: bfloat16 [3072, 2048], P('tp'), may hold values from -0.109375 to 0.109375
- query_key_value_adapter_input: bfloat16 [64, 48, 2048], P('req', None, 'tp'), may hold values from -0.125 to 0.125
- output_adapter_input: bfloat16 [64, 16, 2048], P('req', None, 'tp'), may hold values from -0.125 to 0.125
- gate_up_adapter_input: bfloat16 [64, 32, 2048], P('req', None, 'tp'), may hold values from -0.125 to 0.125
- down_adapter_input: bfloat16 [64, 16, 3072], P('req', None, 'tp'), may hold values from -0.109375 to 0.109375
- query_adapter_output: bfloat16 [64, 16, 2048], P('req', None, 'tp'), may hold values from -1.5 to 1.5
- key_adapter_output: bfloat16 [64, 16, 1024], P('req', None, 'tp'), may hold values from -1.5 to 1.5
- value_adapter_output: bfloat16 [64, 16, 1024], P('req', None, 'tp'), may hold values from -1.5 to 1.5
- projection_adapter_output: bfloat16 [64, 16, 2048], P('req', None, 'tp'), may hold values from -1.5 to 1.5
- gate_adapter_output: bfloat16 [64, 16, 3072], P('req', None, 'tp'), may hold values from -1.5 to 1.5
- up_adapter_output: bfloat16 [64, 16, 3072], P('req', None, 'tp'), may hold values from -1.5 to 1.5
- down_adapter_output: bfloat16 [64, 16, 2048], P('req', None, 'tp'), may hold values from -1.5 to 1.5
Outputs:
- layer_out: bfloat16 [16384, 2048], P('req', 'tp')
Inputs may be any that keep to these rules, and one draw needn't show every extreme that they name: `request_adapter_index`: the 16 requests of one group use adapters of 16 different owners; adapter a belongs to owner a // 2, the index of req that holds it. The lengths of one group's requests sum to 512; the longest is 36.
All inputs are finite; a program needn't handle non-finite values.
Results may differ from a plain program's by a relative error of at most 0.014.
Values may be sent and summed in bfloat16 or wider, within the bound.
A program may use at most 128 MiB of HBM per device.

v0:
```python
import math

import jax
import jax.numpy as jnp
from jax import lax
from jax.sharding import PartitionSpec as P

HEAD_WIDTH = 128


epsilon = 1e-06
rope_base = 1000000.0


def rms_scale(values, gain):
    mean_square = jnp.mean(values * values, axis=-1, keepdims=True)
    return values * lax.rsqrt(mean_square + epsilon) * gain


def rotate(values, position):
    head_size = values.shape[-1]
    half_size = head_size // 2
    inverse = rope_base ** (-(jnp.arange(half_size, dtype=jnp.float32) * 2.0) / head_size)
    angle = position[:, None] * inverse[None, :]
    cosine = jnp.cos(angle)[:, None, :]
    sine = jnp.sin(angle)[:, None, :]
    first_half = values[..., :half_size]
    second_half = values[..., half_size:]
    return jnp.concatenate(
        [first_half * cosine - second_half * sine, second_half * cosine + first_half * sine],
        axis=-1,
    )


def request_layout(request_lens, row_count):
    ends = jnp.cumsum(request_lens)
    starts = ends - request_lens
    row_index = jnp.arange(row_count, dtype=jnp.int32)
    membership_mask = (row_index[:, None] >= starts[None, :]) & (row_index[:, None] < ends[None, :])
    member_int = membership_mask.astype(jnp.int32)
    request = jnp.sum(
        member_int * jnp.arange(request_lens.shape[0], dtype=jnp.int32)[None, :], axis=1
    )
    position = row_index - jnp.sum(member_int * starts[None, :], axis=1)
    return (member_int, request, position, starts)


def attend(query, keys, values, request):
    row_count, query_heads, head_size = query.shape
    kv_heads = keys.shape[1]
    grouped = query.reshape(row_count, kv_heads, query_heads // kv_heads, head_size)
    scores = jnp.einsum(
        "tkgd,skd->kgts", grouped, keys, preferred_element_type=jnp.float32
    ) / math.sqrt(head_size)
    row_index = jnp.arange(row_count, dtype=jnp.int32)
    allowed = (request[:, None] == request[None, :]) & (row_index[None, :] <= row_index[:, None])
    raw = jnp.where(allowed[None, None], jnp.exp(scores), 0.0)
    probs = (raw / jnp.sum(raw, axis=-1, keepdims=True)).astype(jnp.bfloat16)
    mixed = jnp.einsum("kgts,skd->tkgd", probs, values, preferred_element_type=jnp.float32)
    return mixed.reshape(row_count, query_heads * head_size).astype(jnp.bfloat16)


def gather_features(shard):
    return lax.all_gather(shard, "tp", axis=1, tiled=True)


def reduce_columns(term):
    return lax.psum_scatter(term, "tp", scatter_dimension=1, tiled=True)


def expand_low(low_rank, b_tables, form):
    deltas = []
    offset = 0
    for b_table in b_tables:
        rank_width = b_table.shape[1]
        piece = low_rank[..., offset : offset + rank_width]
        deltas.append(
            jnp.einsum(form, piece, b_table, preferred_element_type=jnp.float32).astype(
                jnp.bfloat16
            )
        )
        offset += rank_width
    return deltas


def route_rows(request_lens, starts, owner_of, local_of, member_int, position, owner_adapter_count):
    group_count = lax.axis_size("req")
    row_count = member_int.shape[0]
    request_count = request_lens.shape[0]
    capacity = row_count * 9 // (8 * request_count)
    owner_hit = (owner_of[None, :] == jnp.arange(group_count, dtype=jnp.int32)[:, None]).astype(
        jnp.int32
    )
    first_row = jnp.sum(owner_hit * starts[None, :], axis=1)
    live_count = jnp.sum(owner_hit * request_lens[None, :], axis=1)
    slot_place = jnp.arange(capacity, dtype=jnp.int32)
    slot_valid = slot_place[None, :] < live_count[:, None]
    source_row = jnp.where(slot_valid, first_row[:, None] + slot_place[None, :], 0)
    local_hot = (
        local_of[:, None] == jnp.arange(owner_adapter_count, dtype=jnp.int32)[None, :]
    ).astype(jnp.int32)
    owner_pick = jnp.sum(owner_hit[:, :, None] * local_hot[None, :, :], axis=1)
    pick_flags = (owner_pick[:, None, :] * slot_valid[:, :, None].astype(jnp.int32)).astype(
        jnp.bfloat16
    )
    token_owner = jnp.sum(member_int * owner_of[None, :], axis=1)
    back_index = token_owner * capacity + position
    return (source_row, slot_valid, pick_flags, back_index)


def remote_delta(inputs, a_local, b_locals, plan):
    source_row, slot_valid, pick_flags, back_index = plan
    group_count, capacity = source_row.shape
    picked = jnp.take(inputs, source_row.reshape(-1), axis=0).reshape(
        group_count, capacity, inputs.shape[1]
    )
    picked = jnp.where(slot_valid[:, :, None], picked, jnp.zeros((), inputs.dtype))
    arrived_rows = lax.all_to_all(picked, "req", split_axis=0, concat_axis=0, tiled=True)
    arrived_flags = lax.all_to_all(pick_flags, "req", split_axis=0, concat_axis=0, tiled=True)
    partial_low = jnp.einsum(
        "nkw,arw->nkar", arrived_rows, a_local, preferred_element_type=jnp.float32
    )
    partial_low = jnp.sum(partial_low * arrived_flags.astype(jnp.float32)[:, :, :, None], axis=2)
    low_rank = lax.psum(partial_low, "tp").astype(jnp.bfloat16)
    spread = arrived_flags[:, :, :, None] * low_rank[:, :, None, :]
    joined = jnp.concatenate(expand_low(spread, b_locals, "nkar,aro->nko"), axis=2)
    returned = lax.all_to_all(joined, "req", split_axis=0, concat_axis=0, tiled=True)
    flat_rows = returned.reshape(group_count * capacity, returned.shape[2])
    gathered = jnp.take(flat_rows, back_index, axis=0)
    deltas = []
    offset = 0
    for b_local in b_locals:
        out_width = b_local.shape[2]
        deltas.append(gathered[:, offset : offset + out_width])
        offset += out_width
    return deltas


def per_device(
    tokens,
    lengths,
    request_adapter_index,
    attention_norm_gain,
    query_norm_gain,
    key_norm_gain,
    feedforward_norm_gain,
    query_weight,
    key_weight,
    value_weight,
    output_weight,
    gate_weight,
    up_weight,
    down_weight,
    query_key_value_adapter_input,
    output_adapter_input,
    gate_up_adapter_input,
    down_adapter_input,
    query_adapter_output,
    key_adapter_output,
    value_adapter_output,
    projection_adapter_output,
    gate_adapter_output,
    up_adapter_output,
    down_adapter_output,
):
    row_count = tokens.shape[0]
    feature_width = tokens.shape[1]
    tp_index = lax.axis_index("tp")
    request_lens = lengths[0]
    request_index_list = request_adapter_index[0]
    member_int, request, position, starts = request_layout(request_lens, row_count)
    pos_float = position.astype(jnp.float32)
    owner_adapter_count = query_key_value_adapter_input.shape[0]
    owner_of = request_index_list // owner_adapter_count
    local_of = request_index_list % owner_adapter_count
    adapter_sets = (
        query_key_value_adapter_input,
        output_adapter_input,
        gate_up_adapter_input,
        down_adapter_input,
        query_adapter_output,
        key_adapter_output,
        value_adapter_output,
        projection_adapter_output,
        gate_adapter_output,
        up_adapter_output,
        down_adapter_output,
    )
    plan = route_rows(
        request_lens, starts, owner_of, local_of, member_int, position, owner_adapter_count
    )

    def adapt(inputs, which_a, which_b):
        return remote_delta(
            inputs, adapter_sets[which_a], [adapter_sets[number] for number in which_b], plan
        )

    whole = gather_features(tokens)
    attention_normalized = rms_scale(whole.astype(jnp.float32), attention_norm_gain).astype(
        jnp.bfloat16
    )
    normed_local = lax.dynamic_slice_in_dim(
        attention_normalized, tp_index * feature_width, feature_width, 1
    )
    query_update, key_update, value_update = adapt(normed_local, 0, (4, 5, 6))
    query = jnp.dot(
        attention_normalized, query_weight, preferred_element_type=jnp.float32
    ) + query_update.astype(jnp.float32)
    heads_here = query.shape[1] // HEAD_WIDTH
    query = rotate(
        rms_scale(query.reshape(row_count, heads_here, HEAD_WIDTH), query_norm_gain), pos_float
    ).astype(jnp.bfloat16)
    keys = jnp.dot(
        attention_normalized, key_weight, preferred_element_type=jnp.float32
    ) + key_update.astype(jnp.float32)
    kv_here = keys.shape[1] // HEAD_WIDTH
    keys = rotate(
        rms_scale(keys.reshape(row_count, kv_here, HEAD_WIDTH), key_norm_gain), pos_float
    ).astype(jnp.bfloat16)
    values = (
        jnp.dot(attention_normalized, value_weight, preferred_element_type=jnp.float32)
        + value_update.astype(jnp.float32)
    ).astype(jnp.bfloat16)
    attention_result = attend(query, keys, values.reshape(row_count, kv_here, HEAD_WIDTH), request)
    output_update = adapt(attention_result, 1, (7,))[0]
    summed = reduce_columns(
        jnp.dot(attention_result, output_weight, preferred_element_type=jnp.float32)
    )
    resid = (summed + output_update.astype(jnp.float32) + tokens.astype(jnp.float32)).astype(
        jnp.bfloat16
    )
    whole_two = gather_features(resid)
    feedforward_normalized = rms_scale(whole_two.astype(jnp.float32), feedforward_norm_gain).astype(
        jnp.bfloat16
    )
    normed_two_local = lax.dynamic_slice_in_dim(
        feedforward_normalized, tp_index * feature_width, feature_width, 1
    )
    gate_update, up_update = adapt(normed_two_local, 2, (8, 9))
    gate = jnp.dot(
        feedforward_normalized, gate_weight, preferred_element_type=jnp.float32
    ) + gate_update.astype(jnp.float32)
    upward = jnp.dot(
        feedforward_normalized, up_weight, preferred_element_type=jnp.float32
    ) + up_update.astype(jnp.float32)
    hidden_state = (jax.nn.silu(gate) * upward).astype(jnp.bfloat16)
    down_update = adapt(hidden_state, 3, (10,))[0]
    summed_two = reduce_columns(
        jnp.dot(hidden_state, down_weight, preferred_element_type=jnp.float32)
    )
    return (summed_two + down_update.astype(jnp.float32) + resid.astype(jnp.float32)).astype(
        jnp.bfloat16
    )


def solution(mesh):
    placed = (
        P("req", "tp"),
        P("req", None),
        P("req", None),
        P(),
        P(),
        P(),
        P(),
        P(None, "tp"),
        P(None, "tp"),
        P(None, "tp"),
        P("tp", None),
        P(None, "tp"),
        P(None, "tp"),
        P("tp", None),
        P("req", None, "tp"),
        P("req", None, "tp"),
        P("req", None, "tp"),
        P("req", None, "tp"),
        P("req", None, "tp"),
        P("req", None, "tp"),
        P("req", None, "tp"),
        P("req", None, "tp"),
        P("req", None, "tp"),
        P("req", None, "tp"),
        P("req", None, "tp"),
    )
    return jax.shard_map(
        per_device, mesh=mesh, in_specs=placed, out_specs=P("req", "tp"), check_vma=False
    )
```

profile of v0, /device:TPU:1, one launch (start us, length us, event | category | flops | bytes accessed | tf_op | source)
XLA Modules:
  0.0 581.0 jit_solution(7245208628057516461)
XLA Ops:
  12.0 9.6 %all-to-all-start = ((bf16[32,36,2]{1,2,0:T(2,128)(2,1)}), bf16[32,36,2]{1,2,0:T(2,128)(2,1)S(1)}, u32[]{:S(2)}, u32[]{:S(2)}) async-start(bf16[32,36,2]{1,2,0:T(2,128)(2,1)} %multiply_convert_fusion.1), calls=%async_computation | async-start | bytes 32768 | tf_op jit(solution)/shard_map/all_to_all | solution.py:119
  21.9 20.9 %all-gather.3.cloned.1.call-done = bf16[512,2048]{1,0:T(8,128)(2,1)} async-done(((bf16[512,512]{1,0:T(8,128)(2,1)}), bf16[512,2048]{1,0:T(8,128)(2,1)}) %all-gather.3.cloned.1.call-update) | async-done | bytes 2097168 | tf_op jit(solution)/shard_map/all_gather | solution.py:64
  47.8 5.8 %gather_fusion.3 = bf16[1152,512]{1,0:T(8,128)(2,1)} fusion(bf16[512,512]{1,0:T(8,128)(2,1)} %constant_dynamic-slice_fusion.1, s32[2048]{0:T(1024)S(1)} %pad_clamp_fusion.1), kind=kCustom, calls=%fused_computation.clone | custom fusion | bytes 2363904 | tf_op jit(solution)/shard_map/jit(_take)/gather | solution.py:114
  61.8 8.1 %all-to-all-start.1 = ((bf16[32,36,512]{2,1,0:T(8,128)(2,1)}), bf16[32,36,512]{2,1,0:T(8,128)(2,1)}, u32[]{:S(2)}, u32[]{:S(2)}) async-start(bf16[32,36,512]{2,1,0:T(8,128)(2,1)} %broadcast_select_fusion.3), calls=%async_computation.1 | async-start | bytes 2621440 | tf_op jit(solution)/shard_map/all_to_all | solution.py:118
  69.9 19.3 %all-to-all-done.1 = bf16[32,36,512]{2,1,0:T(8,128)(2,1)} async-done(((bf16[32,36,512]{2,1,0:T(8,128)(2,1)}), bf16[32,36,512]{2,1,0:T(8,128)(2,1)}, u32[]{:S(2)}, u32[]{:S(2)}) %all-to-all-start.1) | async-done | bytes 1179680 | tf_op jit(solution)/shard_map/all_to_all | solution.py:118
  92.0 19.5 %all-reduce.2 = bf16[32,36,48]{2,0,1:T(8,128)(2,1)} all-reduce(f32[32,36,48]{2,0,1:T(8,128)} %copy.69), channel_id=1, replica_groups=mesh['req'=32,'tp'=4] {'tp'}, use_global_device_ids=true, to_apply=%region_8.10 | all-reduce | flops 55296 | bytes 331776 | tf_op jit(solution)/shard_map/psum | solution.py:124
  117.0 8.5 %all-to-all-start.2 = ((bf16[32,36,1024]{2,1,0:T(8,128)(2,1)}), bf16[32,36,1024]{2,1,0:T(8,128)(2,1)}, u32[]{:S(2)}, u32[]{:S(2)}) async-start(bf16[32,36,1024]{2,1,0:T(8,128)(2,1)} %pad_maximum_fusion.1), calls=%async_computation.2 | async-start | bytes 5242880 | tf_op jit(solution)/shard_map/all_to_all | solution.py:127
  129.4 30.1 %all-to-all-done.2 = bf16[32,36,1024]{2,1,0:T(8,128)(2,1)} async-done(((bf16[32,36,1024]{2,1,0:T(8,128)(2,1)}), bf16[32,36,1024]{2,1,0:T(8,128)(2,1)}, u32[]{:S(2)}, u32[]{:S(2)}) %all-to-all-start.2) | async-done | bytes 2359328 | tf_op jit(solution)/shard_map/all_to_all | solution.py:127
  159.5 4.5 reshape.425
  164.1 5.4 gather_fusion
  200.8 5.8 %gather_fusion.4 = bf16[1152,512]{1,0:T(8,128)(2,1)} fusion(bf16[512,512]{1,0:T(8,128)(2,1)} %copy.78, s32[2048]{0:T(1024)S(1)} %copy-done.23), kind=kCustom, calls=%fused_computation.2.clone | custom fusion | bytes 2363904 | tf_op jit(solution)/shard_map/jit(_take)/gather | solution.py:114
  213.8 25.6 %all_to_all.48 = bf16[32,36,512]{2,1,0:T(8,128)(2,1)S(1)} all-to-all(bf16[32,36,512]{2,1,0:T(8,128)(2,1)S(1)} %broadcast_select_fusion.2), channel_id=1, replica_groups=mesh['req'=32,'tp'=4] {'req'}, dimensions={0} | all-to-all | bytes 2359296 | tf_op jit(solution)/shard_map/all_to_all | solution.py:118
  240.5 16.1 %psum.29 = bf16[32,36,16]{1,2,0:T(8,128)(2,1)S(1)} all-reduce(f32[32,36,16]{1,2,0:T(8,128)S(1)} %fusion.28), channel_id=1, replica_groups=mesh['req'=32,'tp'=4] {'tp'}, use_global_device_ids=true, to_apply=%region_15.17 | all-reduce | flops 18432 | bytes 110592 | tf_op jit(solution)/shard_map/psum | solution.py:124
  258.9 8.4 %all-to-all-start.4 = ((bf16[32,36,512]{2,1,0:T(8,128)(2,1)}), bf16[32,36,512]{2,1,0:T(8,128)(2,1)}, u32[]{:S(2)}, u32[]{:S(2)}) async-start(bf16[32,36,512]{2,1,0:T(8,128)(2,1)} %bitcast_convert_fusion.3), calls=%async_computation.5 | async-start | bytes 2621440 | tf_op jit(solution)/shard_map/all_to_all | solution.py:127
  267.4 19.4 %all-to-all-done.4 = bf16[32,36,512]{2,1,0:T(8,128)(2,1)} async-done(((bf16[32,36,512]{2,1,0:T(8,128)(2,1)}), bf16[32,36,512]{2,1,0:T(8,128)(2,1)}, u32[]{:S(2)}, u32[]{:S(2)}) %all-to-all-start.4) | async-done | bytes 1179680 | tf_op jit(solution)/shard_map/all_to_all | solution.py:127
  289.7 4.1 gather_fusion.5
  296.4 27.2 %all-gather.5.cloned.1.call-done = bf16[512,2048]{1,0:T(8,128)(2,1)} async-done(((bf16[512,512]{1,0:T(8,128)(2,1)}), bf16[512,2048]{1,0:T(8,128)(2,1)}) %all-gather.5.cloned.1.call-update) | async-done | bytes 2097168 | tf_op jit(solution)/shard_map/all_gather | solution.py:64
  328.6 5.8 %gather_fusion.6 = bf16[1152,512]{1,0:T(8,128)(2,1)} fusion(bf16[512,512]{1,0:T(8,128)(2,1)} %constant_dynamic-slice_fusion, s32[2048]{0:T(1024)S(1)} %copy-done.24), kind=kCustom, calls=%fused_computation.3.clone | custom fusion | bytes 2363904 | tf_op jit(solution)/shard_map/jit(_take)/gather | solution.py:114
  341.5 27.9 %all_to_all.49 = bf16[32,36,512]{2,1,0:T(8,128)(2,1)S(1)} all-to-all(bf16[32,36,512]{2,1,0:T(8,128)(2,1)S(1)} %broadcast_select_fusion.1), channel_id=1, replica_groups=mesh['req'=32,'tp'=4] {'req'}, dimensions={0} | all-to-all | bytes 2359296 | tf_op jit(solution)/shard_map/all_to_all | solution.py:118
  371.2 18.1 %all-reduce.3 = bf16[32,36,32]{1,2,0:T(8,128)(2,1)S(1)} all-reduce(f32[32,36,32]{1,2,0:T(8,128)} %fusion.17), channel_id=1, replica_groups=mesh['req'=32,'tp'=4] {'tp'}, use_global_device_ids=true, to_apply=%region_18.21 | all-reduce | flops 36864 | bytes 221184 | tf_op jit(solution)/shard_map/psum | solution.py:124
  393.1 8.2 %all-to-all-start.6 = ((bf16[32,36,1536]{2,1,0:T(8,128)(2,1)}), bf16[32,36,1536]{2,1,0:T(8,128)(2,1)}, u32[]{:S(2)}, u32[]{:S(2)}) async-start(bf16[32,36,1536]{2,1,0:T(8,128)(2,1)} %pad_maximum_fusion), calls=%async_computation.7 | async-start | bytes 7864320 | tf_op jit(solution)/shard_map/all_to_all | solution.py:127
  401.3 5.5 fusion.75
  406.7 42.4 %all-to-all-done.6 = bf16[32,36,1536]{2,1,0:T(8,128)(2,1)} async-done(((bf16[32,36,1536]{2,1,0:T(8,128)(2,1)}), bf16[32,36,1536]{2,1,0:T(8,128)(2,1)}, u32[]{:S(2)}, u32[]{:S(2)}) %all-to-all-start.6) | async-done | bytes 3538976 | tf_op jit(solution)/shard_map/all_to_all | solution.py:127
  449.1 5.9 %reshape.432 = bf16[1152,1536]{1,0:T(8,128)(2,1)} reshape(bf16[32,36,1536]{2,1,0:T(8,128)(2,1)} %all-to-all-done.6) | data formatting | bytes 7077888 | tf_op jit(solution)/shard_map/reshape | solution.py:128
  455.0 6.9 %gather_fusion.1 = bf16[512,1536]{1,0:T(8,128)(2,1)} fusion(bf16[1152,1536]{1,0:T(8,128)(2,1)} %reshape.432, s32[1024]{0:T(1024)S(1)} %copy-done.41), kind=kCustom, calls=%fused_computation.6 | custom fusion | bytes 3147776 | tf_op jit(solution)/shard_map/jit(_take)/gather | solution.py:129
  464.0 4.4 multiply_convert_fusion
  469.3 3.8 fusion.76
  473.9 7.0 %gather_fusion.2 = bf16[1152,768]{1,0:T(8,128)(2,1)} fusion(bf16[512,768]{1,0:T(8,128)(2,1)} %copy-done.1, s32[2048]{0:T(1024)S(1)} %pad_clamp_fusion), kind=kCustom, calls=%fused_computation.7 | custom fusion | bytes 3543552 | tf_op jit(solution)/shard_map/jit(_take)/gather | solution.py:114
  486.3 33.2 %all_to_all.50 = bf16[32,36,768]{2,1,0:T(8,128)(2,1)S(1)} all-to-all(bf16[32,36,768]{2,1,0:T(8,128)(2,1)S(1)} %select_select_fusion), channel_id=1, replica_groups=mesh['req'=32,'tp'=4] {'req'}, dimensions={0} | all-to-all | bytes 3538944 | tf_op jit(solution)/shard_map/all_to_all | solution.py:118
  520.9 14.5 %psum.31 = bf16[32,36,16]{1,2,0:T(8,128)(2,1)S(1)} all-reduce(f32[32,36,16]{1,2,0:T(8,128)S(1)} %fusion.31), channel_id=1, replica_groups=mesh['req'=32,'tp'=4] {'tp'}, use_global_device_ids=true, to_apply=%region_21.24 | all-reduce | flops 18432 | bytes 110592 | tf_op jit(solution)/shard_map/psum | solution.py:124
  536.8 27.9 %all_to_all.51 = bf16[32,36,512]{2,1,0:T(8,128)(2,1)} all-to-all(bf16[32,36,512]{2,1,0:T(8,128)(2,1)S(1)} %bitcast_convert_fusion.2), channel_id=1, replica_groups=mesh['req'=32,'tp'=4] {'req'}, dimensions={0} | all-to-all | bytes 2359296 | tf_op jit(solution)/shard_map/all_to_all | solution.py:127
  567.6 4.1 gather_fusion.7
  (219 shorter events, 113.0 us)
Async XLA Ops:
  6.5 462.7 %copy-start = (bf16[768,2048]{1,0:T(8,128)(2,1)S(1)}, bf16[768,2048]{1,0:T(8,128)(2,1)}, u32[]{:S(2)}) copy-start(bf16[768,2048]{1,0:T(8,128)(2,1)} %param.42) | copy-start | bytes 9437188
  6.5 38.5 %copy-start.45 = (f32[2048]{0:T(1024)S(1)}, f32[2048]{0:T(1024)}, u32[]{:S(2)}) copy-start(f32[2048]{0:T(1024)} %param.32) | copy-start | bytes 24580
  6.5 36.3 %all-gather.3.cloned.1.call-start = ((), (), s32[]{:S(2)}) async-start(), calls=%async_computation.11 | async-start | bytes 2621440 | tf_op jit(solution)/shard_map/all_gather | solution.py:64
  9.6 12.2 %copy-start.48 = (s32[16]{0:T(128)}, s32[16]{0:T(128)S(1)}, u32[]{:S(2)}) copy-start(s32[16]{0:T(128)S(1)} %get-tuple-element.30) | copy-start | bytes 196
  11.3 47.8 %copy-start.25 = (pred[32,36]{1,0:T(8,128)(4,1)}, pred[32,36]{1,0:T(8,128)(4,1)S(1)}, u32[]{:S(2)}) copy-start(pred[32,36]{1,0:T(8,128)(4,1)S(1)} %get-tuple-element.22) | copy-start | bytes 3460
  12.0 49.7 %all-to-all-start = ((bf16[32,36,2]{1,2,0:T(2,128)(2,1)}), bf16[32,36,2]{1,2,0:T(2,128)(2,1)S(1)}, u32[]{:S(2)}, u32[]{:S(2)}) async-start(bf16[32,36,2]{1,2,0:T(2,128)(2,1)} %multiply_convert_fusion.1), calls=%async_computation | async-start | bytes 32768 | tf_op jit(solution)/shard_map/all_to_all | solution.py:119
  21.7 23.9 %copy-start.20 = (s32[32,36]{1,0:T(8,128)}, s32[32,36]{1,0:T(8,128)S(1)}, u32[]{:S(2)}) copy-start(s32[32,36]{1,0:T(8,128)S(1)} %add_select_fusion) | copy-start | bytes 13828
  21.9 26.0 %copy-start.22 = (s32[2048]{0:T(1024)}, s32[2048]{0:T(1024)S(1)}, u32[]{:S(2)}) copy-start(s32[2048]{0:T(1024)S(1)} %pad_clamp_fusion.1) | copy-start | bytes 24580
  21.9 31.8 %copy-start.32 = (pred[1152]{0:T(1024)(128)(4,1)}, pred[1152]{0:T(1024)(128)(4,1)S(1)}, u32[]{:S(2)}) copy-start(pred[1152]{0:T(1024)(128)(4,1)S(1)} %compare_and_fusion.1) | copy-start | bytes 3460
  61.8 27.4 %copy-start.56 = (bf16[2,48,512]{2,1,0:T(8,128)(2,1)S(1)}, bf16[2,48,512]{2,1,0:T(8,128)(2,1)}, u32[]{:S(2)}) copy-start(bf16[2,48,512]{2,1,0:T(8,128)(2,1)} %param.43) | copy-start | bytes 294916
  61.8 27.4 %all-to-all-start.1 = ((bf16[32,36,512]{2,1,0:T(8,128)(2,1)}), bf16[32,36,512]{2,1,0:T(8,128)(2,1)}, u32[]{:S(2)}, u32[]{:S(2)}) async-start(bf16[32,36,512]{2,1,0:T(8,128)(2,1)} %broadcast_select_fusion.3), calls=%async_computation.1 | async-start | bytes 2621440 | tf_op jit(solution)/shard_map/all_to_all | solution.py:118
  69.9 22.1 %copy-start.16 = (f32[32,36,2]{1,2,0:T(2,128)}, f32[32,36,2]{1,2,0:T(2,128)S(1)}, u32[]{:S(2)}) copy-start(f32[32,36,2]{1,2,0:T(2,128)S(1)} %convert_element_type.144) | copy-start | bytes 27652
  117.0 8.6 %copy-start.53 = (s32[16]{0:T(128)S(1)}, s32[16]{0:T(128)}, u32[]{:S(2)}) copy-start(s32[16]{0:T(128)} %copy-done.52) | copy-start | bytes 196
  117.0 42.6 %all-to-all-start.2 = ((bf16[32,36,1024]{2,1,0:T(8,128)(2,1)}), bf16[32,36,1024]{2,1,0:T(8,128)(2,1)}, u32[]{:S(2)}, u32[]{:S(2)}) async-start(bf16[32,36,1024]{2,1,0:T(8,128)(2,1)} %pad_maximum_fusion.1), calls=%async_computation.2 | async-start | bytes 5242880 | tf_op jit(solution)/shard_map/all_to_all | solution.py:127
  125.5 168.3 %reduce-scatter.3.cloned.1.call-start = ((), (), s32[]{:S(2)}) async-start(), calls=%async_computation.12 | async-start | bytes 5242880 | tf_op jit(solution)/shard_map/reduce_scatter | solution.py:68
  127.9 36.1 %copy-start.40 = (s32[1024]{0:T(1024)}, s32[1024]{0:T(1024)S(1)}, u32[]{:S(2)}) copy-start(s32[1024]{0:T(1024)S(1)} %pad_clamp_fusion.3) | copy-start | bytes 12292
  128.5 43.4 %copy-start.42 = (pred[512]{0:T(512)(128)(4,1)}, pred[512]{0:T(512)(128)(4,1)S(1)}, u32[]{:S(2)}) copy-start(pred[512]{0:T(512)(128)(4,1)S(1)} %get-tuple-element.12) | copy-start | bytes 1540
  213.8 25.7 %copy-start.17 = (f32[32,36,2]{1,2,0:T(2,128)S(1)}, f32[32,36,2]{1,2,0:T(2,128)}, u32[]{:S(2)}) copy-start(f32[32,36,2]{1,2,0:T(2,128)} %copy-done.16) | copy-start | bytes 27652
  213.8 25.7 %copy-start.31 = (bf16[2,16,512]{2,1,0:T(8,128)(2,1)S(1)}, bf16[2,16,512]{2,1,0:T(8,128)(2,1)}, u32[]{:S(2)}) copy-start(bf16[2,16,512]{2,1,0:T(8,128)(2,1)} %param.44) | copy-start | bytes 98308
  256.5 10.9 %copy-start.47 = (s32[512]{0:T(512)S(1)}, s32[512]{0:T(512)}, u32[]{:S(2)}) copy-start(s32[512]{0:T(512)} %get-tuple-element.13) | copy-start | bytes 6148
  258.9 27.9 %all-to-all-start.4 = ((bf16[32,36,512]{2,1,0:T(8,128)(2,1)}), bf16[32,36,512]{2,1,0:T(8,128)(2,1)}, u32[]{:S(2)}, u32[]{:S(2)}) async-start(bf16[32,36,512]{2,1,0:T(8,128)(2,1)} %bitcast_convert_fusion.3), calls=%async_computation.5 | async-start | bytes 2621440 | tf_op jit(solution)/shard_map/all_to_all | solution.py:127
  267.3 56.2 %all-gather.5.cloned.1.call-start = ((), (), s32[]{:S(2)}) async-start(), calls=%async_computation.13 | async-start | bytes 2621440 | tf_op jit(solution)/shard_map/all_gather | solution.py:64
  267.4 26.4 %copy-start.37 = (s32[1024]{0:T(1024)}, s32[1024]{0:T(1024)S(1)}, u32[]{:S(2)}) copy-start(s32[1024]{0:T(1024)S(1)} %pad_clamp_fusion.2) | copy-start | bytes 12292
  296.4 29.4 %copy-start.46 = (f32[2048]{0:T(1024)S(1)}, f32[2048]{0:T(1024)}, u32[]{:S(2)}) copy-start(f32[2048]{0:T(1024)} %param.35) | copy-start | bytes 24580
  341.5 27.9 %copy-start.18 = (f32[32,36,2]{1,2,0:T(2,128)S(1)}, f32[32,36,2]{1,2,0:T(2,128)}, u32[]{:S(2)}) copy-start(f32[32,36,2]{1,2,0:T(2,128)} %copy-done.16) | copy-start | bytes 27652
  341.5 27.9 %copy-start.57 = (bf16[2,32,512]{2,1,0:T(8,128)(2,1)S(1)}, bf16[2,32,512]{2,1,0:T(8,128)(2,1)}, u32[]{:S(2)}) copy-start(bf16[2,32,512]{2,1,0:T(8,128)(2,1)} %param.45) | copy-start | bytes 196612
  369.4 20.0 %copy-start.28 = (bf16[2,16,768]{2,1,0:T(8,128)(2,1)S(1)}, bf16[2,16,768]{2,1,0:T(8,128)(2,1)}, u32[]{:S(2)}) copy-start(bf16[2,16,768]{2,1,0:T(8,128)(2,1)} %param.52) | copy-start | bytes 147460
  393.1 56.1 %all-to-all-start.6 = ((bf16[32,36,1536]{2,1,0:T(8,128)(2,1)}), bf16[32,36,1536]{2,1,0:T(8,128)(2,1)}, u32[]{:S(2)}, u32[]{:S(2)}) async-start(bf16[32,36,1536]{2,1,0:T(8,128)(2,1)} %pad_maximum_fusion), calls=%async_computation.7 | async-start | bytes 7864320 | tf_op jit(solution)/shard_map/all_to_all | solution.py:127
  401.2 170.5 %reduce-scatter.5.cloned.1.call-start = ((), (), s32[]{:S(2)}) async-start(), calls=%async_computation.14 | async-start | bytes 5242880 | tf_op jit(solution)/shard_map/reduce_scatter | solution.py:68
  406.7 48.3 %copy-start.41 = (s32[1024]{0:T(1024)S(1)}, s32[1024]{0:T(1024)}, u32[]{:S(2)}) copy-start(s32[1024]{0:T(1024)} %copy-done.40) | copy-start | bytes 12292
  486.3 33.2 %copy-start.30 = (bf16[2,16,768]{2,1,0:T(8,128)(2,1)S(1)}, bf16[2,16,768]{2,1,0:T(8,128)(2,1)}, u32[]{:S(2)}) copy-start(bf16[2,16,768]{2,1,0:T(8,128)(2,1)} %param.46) | copy-start | bytes 147460
  536.8 30.9 %copy-start.38 = (s32[1024]{0:T(1024)S(1)}, s32[1024]{0:T(1024)}, u32[]{:S(2)}) copy-start(s32[1024]{0:T(1024)} %copy-done.37) | copy-start | bytes 12292
  (35 other events, 100.7 us)
Sparse Core Ops, SparseCore 0:
  9.0 33.7 all-gather.2
  198.9 44.6 reduce-scatter.2
  296.5 26.9 all-gather.4
  473.2 44.4 reduce-scatter.4
where the time goes:
time: 590 us; the launch traced here: 581 us
  blocking collectives  183 us (31%)
  waiting for transfers between devices  160 us (27%)
  local copies, waits for them, and re-layouts  97.6 us (17%)
  starting transfers between devices  42.9 us (7%)
  matrix products  42.5 us (7%)
  other arithmetic  41 us (7%)
  between operations  14.1 us (2%)
    all_to_all x3, waiting for transfers between devices, remote_delta(): lax.all_to_all(joined, 'req', split_axis=0, concat_axis=0, tiled=True)  91.9 us
    all_to_all x3, blocking collectives, remote_delta(): lax.all_to_all(picked, 'req', split_axis=0, concat_axis=0, tiled=True)  86.8 us
    psum x4, blocking collectives, remote_delta(): low_rank = lax.psum(partial_low, 'tp').astype(jnp.bfloat16)  68.2 us
    all_gather x2, waiting for transfers between devices, gather_features(): return lax.all_gather(shard, 'tp', axis=1, tiled=True)  48.1 us
    gather x5, local copies, waits for them, and re-layouts, remote_delta(): jnp.take(inputs, source_row.reshape(-1), axis=0)  28.1 us
    all_to_all x1, blocking collectives, remote_delta(): lax.all_to_all(joined, 'req', split_axis=0, concat_axis=0, tiled=True)  27.9 us
    all_to_all x3, starting transfers between devices, remote_delta(): lax.all_to_all(joined, 'req', split_axis=0, concat_axis=0, tiled=True)  25.1 us
    gather x5, local copies, waits for them, and re-layouts, remote_delta(): gathered = jnp.take(flat_rows, back_index, axis=0)  22.8 us
  transfers between devices with their start and end apart: 9, of which 6 were waited for; matrix products, arithmetic and copies ran while one was open for 14% of the time, Pallas kernels for 0%

commit v1 on v0

v1 whole, which is shorter than its diff:
```python
import math

import jax
import jax.numpy as jnp
from jax import lax
from jax.experimental import pallas as pl
from jax.experimental.pallas import tpu as pltpu
from jax.sharding import PartitionSpec as P

HEAD_WIDTH = 128


epsilon = 1e-06
rope_base = 1000000.0


def rms_scale(values, gain):
    mean_square = jnp.mean(values * values, axis=-1, keepdims=True)
    return values * lax.rsqrt(mean_square + epsilon) * gain


def rotate(values, position):
    head_size = values.shape[-1]
    half_size = head_size // 2
    inverse = rope_base ** (-(jnp.arange(half_size, dtype=jnp.float32) * 2.0) / head_size)
    angle = position[:, None] * inverse[None, :]
    cosine = jnp.cos(angle)[:, None, :]
    sine = jnp.sin(angle)[:, None, :]
    first_half = values[..., :half_size]
    second_half = values[..., half_size:]
    return jnp.concatenate(
        [first_half * cosine - second_half * sine, second_half * cosine + first_half * sine],
        axis=-1,
    )


def request_layout(request_lens, row_count):
    ends = jnp.cumsum(request_lens)
    starts = ends - request_lens
    row_index = jnp.arange(row_count, dtype=jnp.int32)
    membership_mask = (row_index[:, None] >= starts[None, :]) & (row_index[:, None] < ends[None, :])
    member_int = membership_mask.astype(jnp.int32)
    request = jnp.sum(
        member_int * jnp.arange(request_lens.shape[0], dtype=jnp.int32)[None, :], axis=1
    )
    position = row_index - jnp.sum(member_int * starts[None, :], axis=1)
    return (member_int, request, position, starts)


def attend(query, keys, values, request):
    row_count, query_heads, head_size = query.shape
    kv_heads = keys.shape[1]
    grouped = query.reshape(row_count, kv_heads, query_heads // kv_heads, head_size)
    scores = jnp.einsum(
        "tkgd,skd->kgts", grouped, keys, preferred_element_type=jnp.float32
    ) / math.sqrt(head_size)
    row_index = jnp.arange(row_count, dtype=jnp.int32)
    allowed = (request[:, None] == request[None, :]) & (row_index[None, :] <= row_index[:, None])
    raw = jnp.where(allowed[None, None], jnp.exp(scores), 0.0)
    probs = (raw / jnp.sum(raw, axis=-1, keepdims=True)).astype(jnp.bfloat16)
    mixed = jnp.einsum("kgts,skd->tkgd", probs, values, preferred_element_type=jnp.float32)
    return mixed.reshape(row_count, query_heads * head_size).astype(jnp.bfloat16)


def gather_features(shard):
    return lax.all_gather(shard, "tp", axis=1, tiled=True)


def reduce_columns(term):
    return lax.psum_scatter(term, "tp", scatter_dimension=1, tiled=True)


def pick_kernel(pick_ref, table_ref, *out_refs):
    offset = 0
    for out_ref in out_refs:
        rows = out_ref.shape[1]
        out_ref[...] = table_ref[:, offset : offset + rows, :]
        offset += rows


def pick_adapters(table, index_list, row_counts):
    count = index_list.shape[0]
    rows, width = table.shape[1:]
    grid_spec = pltpu.PrefetchScalarGridSpec(
        num_scalar_prefetch=1,
        grid=(count,),
        in_specs=[pl.BlockSpec((1, rows, width), lambda i, pick: (pick[i], 0, 0))],
        out_specs=[pl.BlockSpec((1, n, width), lambda i, pick: (i, 0, 0)) for n in row_counts],
    )
    picked = pl.pallas_call(
        pick_kernel,
        grid_spec=grid_spec,
        out_shape=[jax.ShapeDtypeStruct((count, n, width), table.dtype) for n in row_counts],
        compiler_params=pltpu.CompilerParams(vmem_limit_bytes=8 << 20),
    )(index_list, table)
    return [part.reshape(-1, width) for part in picked]


def gather_owned(parts):
    return lax.all_gather(jnp.concatenate(parts, axis=1), "req", axis=0, tiled=True)


def low_product(inputs, a_rows, own):
    low = lax.dot_general(
        inputs, a_rows, (((1,), (1,)), ((), ())), preferred_element_type=jnp.float32
    )
    return jnp.where(own, low, 0.0).astype(jnp.bfloat16)


def product(left, right):
    return jnp.dot(left, right, preferred_element_type=jnp.float32)


def per_device(
    tokens,
    lengths,
    request_adapter_index,
    attention_norm_gain,
    query_norm_gain,
    key_norm_gain,
    feedforward_norm_gain,
    query_weight,
    key_weight,
    value_weight,
    output_weight,
    gate_weight,
    up_weight,
    down_weight,
    query_key_value_adapter_input,
    output_adapter_input,
    gate_up_adapter_input,
    down_adapter_input,
    query_adapter_output,
    key_adapter_output,
    value_adapter_output,
    projection_adapter_output,
    gate_adapter_output,
    up_adapter_output,
    down_adapter_output,
):
    row_count = tokens.shape[0]
    request_lens = lengths[0]
    request_index_list = request_adapter_index[0]
    member_int, request, position, starts = request_layout(request_lens, row_count)
    pos_float = position.astype(jnp.float32)
    rank = query_adapter_output.shape[1]
    request_count = request_lens.shape[0]
    column_request = jnp.arange(request_count * rank, dtype=jnp.int32) // rank
    own = request[:, None] == column_request[None, :]

    whole = gather_features(tokens)
    table_one = gather_owned(
        [
            query_key_value_adapter_input,
            query_adapter_output,
            jnp.concatenate([key_adapter_output, value_adapter_output], axis=2),
        ]
    )
    table_two = gather_owned(
        [
            output_adapter_input,
            projection_adapter_output,
            gate_up_adapter_input,
            down_adapter_output,
        ]
    )
    table_three = gather_owned([gate_adapter_output, up_adapter_output, down_adapter_input])
    a_qkv, b_query, b_kv = pick_adapters(table_one, request_index_list, (3 * rank, rank, rank))
    a_qkv = gather_features(a_qkv)
    a_out, b_out, a_gate_up, b_down = pick_adapters(
        table_two, request_index_list, (rank, rank, 2 * rank, rank)
    )
    b_gate, b_up, a_down = pick_adapters(table_three, request_index_list, (rank, rank, rank))
    spread = gather_features(
        jnp.concatenate([a_gate_up, b_out, b_down], axis=0)
    )
    pair_rows = 2 * rank * request_count
    single_rows = rank * request_count
    a_gate_up = spread[:pair_rows].reshape(request_count, 2, rank, -1)
    b_out = spread[pair_rows : pair_rows + single_rows]
    b_down = spread[pair_rows + single_rows :]
    a_qkv = a_qkv.reshape(request_count, 3, rank, -1)

    def part(stack, number):
        return stack[:, number].reshape(single_rows, -1)

    normed = rms_scale(whole.astype(jnp.float32), attention_norm_gain).astype(jnp.bfloat16)
    kv_width = key_weight.shape[1]
    query = product(normed, query_weight) + product(
        low_product(normed, part(a_qkv, 0), own), b_query
    )
    heads_here = query.shape[1] // HEAD_WIDTH
    query = rotate(
        rms_scale(query.reshape(row_count, heads_here, HEAD_WIDTH), query_norm_gain), pos_float
    ).astype(jnp.bfloat16)
    keys = product(normed, key_weight) + product(
        low_product(normed, part(a_qkv, 1), own), b_kv[:, :kv_width]
    )
    kv_here = keys.shape[1] // HEAD_WIDTH
    keys = rotate(
        rms_scale(keys.reshape(row_count, kv_here, HEAD_WIDTH), key_norm_gain), pos_float
    ).astype(jnp.bfloat16)
    values = (
        product(normed, value_weight)
        + product(low_product(normed, part(a_qkv, 2), own), b_kv[:, kv_width:])
    ).astype(jnp.bfloat16)
    attended = attend(query, keys, values.reshape(row_count, kv_here, HEAD_WIDTH), request)
    share = product(attended, output_weight) + product(low_product(attended, a_out, own), b_out)
    summed = reduce_columns(share.astype(jnp.bfloat16))
    resid = (summed.astype(jnp.float32) + tokens.astype(jnp.float32)).astype(jnp.bfloat16)
    whole_two = gather_features(resid)
    normed_two = rms_scale(whole_two.astype(jnp.float32), feedforward_norm_gain).astype(
        jnp.bfloat16
    )
    gate = product(normed_two, gate_weight) + product(
        low_product(normed_two, part(a_gate_up, 0), own), b_gate
    )
    upward = product(normed_two, up_weight) + product(
        low_product(normed_two, part(a_gate_up, 1), own), b_up
    )
    hidden = (jax.nn.silu(gate) * upward).astype(jnp.bfloat16)
    share_two = product(hidden, down_weight) + product(low_product(hidden, a_down, own), b_down)
    summed_two = reduce_columns(share_two.astype(jnp.bfloat16))
    return (summed_two.astype(jnp.float32) + resid.astype(jnp.float32)).astype(jnp.bfloat16)


def solution(mesh):
    placed = (
        P("req", "tp"),
        P("req", None),
        P("req", None),
        P(),
        P(),
        P(),
        P(),
        P(None, "tp"),
        P(None, "tp"),
        P(None, "tp"),
        P("tp", None),
        P(None, "tp"),
        P(None, "tp"),
        P("tp", None),
        P("req", None, "tp"),
        P("req", None, "tp"),
        P("req", None, "tp"),
        P("req", None, "tp"),
        P("req", None, "tp"),
        P("req", None, "tp"),
        P("req", None, "tp"),
        P("req", None, "tp"),
        P("req", None, "tp"),
        P("req", None, "tp"),
        P("req", None, "tp"),
    )
    return jax.shard_map(
        per_device, mesh=mesh, in_specs=placed, out_specs=P("req", "tp"), check_vma=False
    )
```

time: 590 us -> 423 us (0.72); the launches traced: 581 us -> 422 us
  blocking collectives: 183 us -> 0 us
  waiting for transfers between devices: 160 us -> 290 us
  local copies, waits for them, and re-layouts: 97.6 us -> 28.5 us
  starting transfers between devices: 42.9 us -> 0.33 us
  matrix products: 42.5 us -> 64.4 us
  other arithmetic: 41 us -> 22.6 us
    all_gather x0 -> x3, waiting for transfers between devices: none -> 136 us  [gather_owned(): lax.all_gather(jnp.concatenate(parts, axis=1), 'req', axis=0, tiled=True)]
    all_to_all x4 -> x0, blocking collectives: 115 us -> none  [the longest x3 86.8 us: remote_delta(): lax.all_to_all(picked, 'req', split_axis=0, concat_axis=0, tiled=True)]
    all_to_all x5 -> x0, waiting for transfers between devices: 111 us -> none  [the longest x3 91.9 us: remote_delta(): lax.all_to_all(joined, 'req', split_axis=0, concat_axis=0, tiled=True)]
    psum x4 -> x0, blocking collectives: 68.2 us -> none  [remote_delta(): low_rank = lax.psum(partial_low, 'tp').astype(jnp.bfloat16)]
    reduce_scatter x2, waiting for transfers between devices: 0.01 us -> 58.7 us  [reduce_columns(): return lax.psum_scatter(term, 'tp', scatter_dimension=1, tiled=True)]
    gather x10 -> x0, local copies, waits for them, and re-layouts: 50.9 us -> none  [the longest x5 28.1 us: remote_delta(): jnp.take(inputs, source_row.reshape(-1), axis=0)]
    all_gather x2 -> x4, waiting for transfers between devices: 48.1 us -> 95 us  [gather_features(): return lax.all_gather(shard, 'tp', axis=1, tiled=True)]
    all_to_all x5 -> x0, starting transfers between devices: 42.7 us -> none  [the longest x3 25.1 us: remote_delta(): lax.all_to_all(joined, 'req', split_axis=0, concat_axis=0, tiled=True)]
  transfers between devices with their start and end apart: 9 -> 9, of which waited for: 6 -> 9; matrix products, arithmetic and copies ran while one was open for 14% -> 13% of each run, Pallas kernels for 0% -> 1%
where the time goes in v1:
time: 423 us; the launch traced here: 422 us
  waiting for transfers between devices  290 us (69%)
  matrix products  64.4 us (15%)
  local copies, waits for them, and re-layouts  28.5 us (7%)
  other arithmetic  22.6 us (5%)
  between operations  13.5 us (3%)
    all_gather x3, waiting for transfers between devices, gather_owned(): lax.all_gather(jnp.concatenate(parts, axis=1), 'req', axis=0, tiled=True)  136 us
    all_gather x4, waiting for transfers between devices, gather_features(): return lax.all_gather(shard, 'tp', axis=1, tiled=True)  95 us
    dot_general x14, matrix products, product(): return jnp.dot(left, right, preferred_element_type=jnp.float32)  60.7 us
    reduce_scatter x2, waiting for transfers between devices, reduce_columns(): return lax.psum_scatter(term, 'tp', scatter_dimension=1, tiled=True)  58.7 us
    unnamed x62, local copies, waits for them, and re-layouts  14 us
  transfers between devices with their start and end apart: 9, of which 9 were waited for; matrix products, arithmetic and copies ran while one was open for 13% of the time, Pallas kernels for 1%

profile of v1, /device:TPU:1, one launch (start us, length us, event | category | flops | bytes accessed | tf_op | source)
XLA Modules:
  0.0 422.1 jit_solution(12635172555203551339)
XLA Ops:
  10.7 49.9 %all-gather.10.cloned.1.call-done.table_ref = bf16[64,80,512]{2,1,0:T(8,128)(2,1)} async-done(((bf16[2,80,512]{2,1,0:T(8,128)(2,1)}), bf16[64,80,512]{2,1,0:T(8,128)(2,1)}) %all-gather.10.cloned.1.call-update) | async-done | bytes 5242896 | tf_op jit(solution)/shard_map/all_gather | solution.py:100
  60.6 2.5 copy-done.2
  70.5 38.8 %all-gather.14.cloned.1.call-done.table_ref = bf16[64,80,512]{2,1,0:T(8,128)(2,1)} async-done(((bf16[2,80,512]{2,1,0:T(8,128)(2,1)}), bf16[64,80,512]{2,1,0:T(8,128)(2,1)}) %all-gather.14.cloned.1.call-update) | async-done | bytes 5242896 | tf_op jit(solution)/shard_map/all_gather | solution.py:100
  109.3 2.5 copy-done.1
  113.9 26.4 %all-gather.8.cloned.1.call-done = bf16[512,2048]{1,0:T(8,128)(2,1)} async-done(((bf16[512,512]{1,0:T(8,128)(2,1)}), bf16[512,2048]{1,0:T(8,128)(2,1)}) %all-gather.8.cloned.1.call-update) | async-done | bytes 2097168 | tf_op jit(solution)/shard_map/all_gather | solution.py:66
  140.2 2.2 fusion
  145.3 2.3 fusion.75
  147.6 33.7 %all-gather.12.cloned.1.call-done = bf16[768,2048]{1,0:T(8,128)(2,1)} async-done(((bf16[768,512]{1,0:T(8,128)(2,1)}), bf16[768,2048]{1,0:T(8,128)(2,1)}) %all-gather.12.cloned.1.call-update) | async-done | bytes 3145744 | tf_op jit(solution)/shard_map/all_gather | solution.py:66
  181.3 3.6 fusion.73
  184.9 3.7 fusion.17
  188.6 4.1 multiply_reduce_fusion.1
  194.8 4.6 %multiply_reduce_fusion = (f32[512,4]{0,1:T(4,128)S(1)}, f32[512,512]{0,1:T(8,128)}) fusion(f32[512,512]{0,1:T(8,128)} %fusion.75, bf16[256,512]{1,0:T(8,128)(2,1)} %bitcast.88, bf16[512,2048]{1,0:T(8,128)(2,1)} %copy-done.11, bf16[256,2048]{1,0:T(8,128)(2,1)} %bitcast.99, s32[256]{0:T(256)} %copy-done.25, s32[512]{0:T(512)S(1)} %get-tuple-element.26), kind=kOutput, calls=%fused_computation.46 | convolution fusion | flops 672266240 | bytes 5516288 | tf_op jit(solution)/shard_map/dot_general | solution.py:111
  209.2 3.8 fusion.18
  213.0 2.9 fusion.9
  217.5 2.1 fusion.8
  219.6 11.6 %all-gather.16.cloned.1.call-done = bf16[1024,2048]{1,0:T(8,128)(2,1)} async-done(((bf16[1024,512]{1,0:T(8,128)(2,1)}), bf16[1024,2048]{1,0:T(8,128)(2,1)}) %all-gather.16.cloned.1.call-update) | async-done | bytes 4194320 | tf_op jit(solution)/shard_map/all_gather | solution.py:66
  231.2 4.6 %fusion.20 = f32[512,2048]{1,0:T(8,128)} fusion(bf16[512,512]{0,1:T(8,128)(2,1)} %bitcast.100, bf16[256,512]{1,0:T(8,128)(2,1)S(1)} %bitcast.87, bf16[1024,2048]{1,0:T(8,128)(2,1)} %all-gather.16.cloned.1.call-done, s32[256]{0:T(256)S(1)} %copy-done.26, s32[512]{0:T(512)S(1)} %get-tuple-element.26), kind=kOutput, calls=%fused_computation.39 | convolution fusion | flops 671481856 | bytes 6032384 | tf_op jit(solution)/shard_map/dot_general | solution.py:111
  235.8 5.9 %add_convert_fusion.1 = bf16[512,2048]{1,0:T(8,128)(2,1)} fusion(f32[512,2048]{1,0:T(8,128)} %fusion.20, bf16[512,512]{0,1:T(8,128)(2,1)} %bitcast.101, bf16[512,2048]{1,0:T(8,128)(2,1)} %param.35), kind=kOutput, calls=%fused_computation.12 | convolution fusion | flops 1075838976 | bytes 8912896 | tf_op jit(solution)/shard_map/dot_general | solution.py:111
  243.2 28.7 %reduce-scatter.3.cloned.1.call-done = bf16[512,512]{1,0:T(8,128)(2,1)} async-done(((bf16[512,2048]{1,0:T(8,128)(2,1)}), bf16[512,512]{1,0:T(8,128)(2,1)}) %reduce-scatter.3.cloned.1.call-update) | async-done | bytes 524304 | tf_op jit(solution)/shard_map/reduce_scatter | solution.py:70
  272.0 2.1 add_convert_fusion.3
  274.2 47.1 %all-gather.20.cloned.1.call-done.table_ref = bf16[64,48,768]{2,1,0:T(8,128)(2,1)} async-done(((bf16[2,48,768]{2,1,0:T(8,128)(2,1)}), bf16[64,48,768]{2,1,0:T(8,128)(2,1)}) %all-gather.20.cloned.1.call-update) | async-done | bytes 4718608 | tf_op jit(solution)/shard_map/all_gather | solution.py:100
  321.3 2.3 copy-done.3
  329.0 23.4 %all-gather.18.cloned.1.call-done = bf16[512,2048]{1,0:T(8,128)(2,1)} async-done(((bf16[512,512]{1,0:T(8,128)(2,1)}), bf16[512,2048]{1,0:T(8,128)(2,1)}) %all-gather.18.cloned.1.call-update) | async-done | bytes 2097168 | tf_op jit(solution)/shard_map/all_gather | solution.py:66
  352.4 2.2 fusion.3
  354.7 5.2 %fusion.67 = f32[512,768]{1,0:T(8,128)} fusion(bf16[2048,768]{1,0:T(8,128)(2,1)} %param.37, bf16[512,2048]{1,0:T(8,128)(2,1)S(1)} %copy-done.13, f32[2048]{0:T(1024)} %param.31, f32[512]{0:T(512)S(1)} %add_rsqrt_fusion.2), kind=kOutput, calls=%fused_computation.117 | convolution fusion | flops 1614807040 | bytes 6825984 | tf_op jit(solution)/shard_map/dot_general | solution.py:111
  359.9 3.0 fusion.71
  362.9 4.5 %fusion.19 = f32[512,768]{1,0:T(8,128)} fusion(bf16[256,768]{1,0:T(8,128)(2,1)} %bitcast.95, bf16[256,2048]{1,0:T(8,128)(2,1)} %bitcast.106, s32[256]{0:T(256)S(1)} %copy-done.26, s32[512]{0:T(512)S(1)} %get-tuple-element.26, bf16[512,2048]{1,0:T(8,128)(2,1)} %all-gather.18.cloned.1.call-done, f32[2048]{0:T(1024)} %param.31, f32[512]{0:T(512)S(1)} %add_rsqrt_fusion.2), kind=kOutput, calls=%fused_computation.38 | convolution fusion | flops 742785024 | bytes 5125120 | tf_op jit(solution)/shard_map/dot_general | solution.py:111
  367.3 5.7 %multiply_convert_fusion = bf16[512,768]{1,0:T(8,128)(2,1)} fusion(f32[512,768]{1,0:T(8,128)} %fusion.67, f32[512,768]{1,0:T(8,128)} %fusion.71, f32[512,768]{1,0:T(8,128)} %fusion.19, bf16[256,768]{1,0:T(8,128)(2,1)} %bitcast.94, bf16[256,2048]{1,0:T(8,128)(2,1)} %bitcast.105, s32[256]{0:T(256)S(1)} %copy-done.26, s32[512]{0:T(512)S(1)} %get-tuple-element.26, ...), kind=kOutput, calls=%fused_computation.16 | convolution fusion | flops 745930752 | bytes 9057280 | tf_op jit(solution)/shard_map/dot_general | solution.py:111
  373.0 4.9 %fusion.76 = f32[512,2048]{1,0:T(8,128)} fusion(bf16[512,768]{1,0:T(8,128)(2,1)} %multiply_convert_fusion, bf16[768,2048]{1,0:T(8,128)(2,1)S(1)} %copy-done), kind=kOutput, calls=%fused_computation.122 | convolution fusion | flops 1610612736 | bytes 8126464 | tf_op jit(solution)/shard_map/dot_general | solution.py:111
  378.0 5.5 %add_convert_fusion = bf16[512,2048]{1,0:T(8,128)(2,1)} fusion(f32[512,2048]{1,0:T(8,128)} %fusion.76, bf16[512,768]{1,0:T(8,128)(2,1)} %multiply_convert_fusion, bf16[256,768]{1,0:T(8,128)(2,1)S(1)} %bitcast.86, bf16[1024,2048]{1,0:T(8,128)(2,1)} %all-gather.16.cloned.1.call-done, s32[256]{0:T(256)S(1)} %copy-done.26, s32[512]{0:T(512)S(1)} %get-tuple-element.26), kind=kOutput, calls=%fused_computation.11 | convolution fusion | flops 740687872 | bytes 8522752 | tf_op jit(solution)/shard_map/dot_general | solution.py:111
  383.5 30.0 %reduce-scatter.5.cloned.1.call-done = bf16[512,512]{1,0:T(8,128)(2,1)} async-done(((bf16[512,2048]{1,0:T(8,128)(2,1)}), bf16[512,512]{1,0:T(8,128)(2,1)}) %reduce-scatter.5.cloned.1.call-update) | async-done | bytes 524304 | tf_op jit(solution)/shard_map/reduce_scatter | solution.py:70
  413.5 2.1 add_convert_fusion.2
  (112 shorter events, 36.8 us)
Async XLA Ops:
  6.5 366.5 %copy-start = (bf16[768,2048]{1,0:T(8,128)(2,1)S(1)}, bf16[768,2048]{1,0:T(8,128)(2,1)}, u32[]{:S(2)}) copy-start(bf16[768,2048]{1,0:T(8,128)(2,1)} %param.38) | copy-start | bytes 9437188
  6.5 54.1 %all-gather.10.cloned.1.call-start = ((), (), s32[]{:S(2)}) async-start(), calls=%async_computation.3 | async-start | bytes 5406720 | tf_op jit(solution)/shard_map/all_gather | solution.py:100
  8.3 101.0 %all-gather.14.cloned.1.call-start = ((), (), s32[]{:S(2)}) async-start(), calls=%async_computation.5 | async-start | bytes 5406720 | tf_op jit(solution)/shard_map/all_gather | solution.py:100
  10.0 130.3 %all-gather.8.cloned.1.call-start = ((), (), s32[]{:S(2)}) async-start(), calls=%async_computation.2 | async-start | bytes 2621440 | tf_op jit(solution)/shard_map/all_gather | solution.py:66
  10.7 170.6 %all-gather.12.cloned.1.call-start = ((), (), s32[]{:S(2)}) async-start(), calls=%async_computation.4 | async-start | bytes 3932160 | tf_op jit(solution)/shard_map/all_gather | solution.py:66
  60.6 2.5 copy-start.2
  63.7 3.3 copy-start.27
  67.0 42.4 %copy-start.7 = (s32[1,16]{1,0:T(1,128)S(1)}, s32[1,16]{1,0:T(1,128)}, u32[]{:S(2)}) copy-start(s32[1,16]{1,0:T(1,128)} %param.27) | copy-start | bytes 196
  67.0 164.2 %all-gather.16.cloned.1.call-start = ((), (), s32[]{:S(2)}) async-start(), calls=%async_computation.6 | async-start | bytes 5242880 | tf_op jit(solution)/shard_map/all_gather | solution.py:66
  68.0 2.6 copy-start.14
  109.3 2.5 copy-start.1
  113.8 158.2 %reduce-scatter.3.cloned.1.call-start = ((), (), s32[]{:S(2)}) async-start(), calls=%async_computation.7 | async-start | bytes 2621440 | tf_op jit(solution)/shard_map/reduce_scatter | solution.py:70
  113.9 71.0 %copy-start.25 = (s32[256]{0:T(256)}, s32[256]{0:T(256)S(1)}, u32[]{:S(2)}) copy-start(s32[256]{0:T(256)S(1)} %and_select_fusion) | copy-start | bytes 3076
  140.2 2.2 copy-start.12
  142.5 2.8 copy-start.29
  143.9 1.4 copy-start.11
  199.5 1.4 copy-start.15
  200.9 5.0 %copy-start.24 = (f32[512,2]{0,1:T(2,128)S(1)}, f32[512,2]{0,1:T(2,128)}, u32[]{:S(2)}) copy-start(f32[512,2]{0,1:T(2,128)} %get-tuple-element.40) | copy-start | bytes 12292
  203.9 5.3 %copy-start.26 = (s32[256]{0:T(256)S(1)}, s32[256]{0:T(256)}, u32[]{:S(2)}) copy-start(s32[256]{0:T(256)} %copy-done.25) | copy-start | bytes 3076
  213.0 2.9 copy-start.16
  213.0 2.9 copy-start.17
  213.0 2.9 copy-start.18
  213.0 2.9 copy-start.19
  213.0 2.9 copy-start.20
  241.7 79.6 %all-gather.20.cloned.1.call-start = ((), (), s32[]{:S(2)}) async-start(), calls=%async_computation.9 | async-start | bytes 4866048 | tf_op jit(solution)/shard_map/all_gather | solution.py:100
  243.2 109.2 %all-gather.18.cloned.1.call-start = ((), (), s32[]{:S(2)}) async-start(), calls=%async_computation.8 | async-start | bytes 2621440 | tf_op jit(solution)/shard_map/all_gather | solution.py:66
  274.1 139.3 %reduce-scatter.5.cloned.1.call-start = ((), (), s32[]{:S(2)}) async-start(), calls=%async_computation.10 | async-start | bytes 2621440 | tf_op jit(solution)/shard_map/reduce_scatter | solution.py:70
  321.3 2.3 copy-start.3
  326.0 1.6 slice-start
  352.4 2.2 copy-start.13
  354.6 5.2 %copy-start.28 = (bf16[2048,768]{1,0:T(8,128)(2,1)S(1)}, bf16[2048,768]{1,0:T(8,128)(2,1)}, u32[]{:S(2)}) copy-start(bf16[2048,768]{1,0:T(8,128)(2,1)} %param.36) | copy-start | bytes 9437188
  354.7 5.2 %copy-start.30 = (f32[2048]{0:T(1024)S(1)}, f32[2048]{0:T(1024)}, u32[]{:S(2)}) copy-start(f32[2048]{0:T(1024)} %param.31) | copy-start | bytes 24580
  (9 other events, 6.9 us)
Sparse Core Ops, SparseCore 0:
  9.6 50.9 all-gather.9
  62.8 46.4 all-gather.13
  111.0 29.2 all-gather.7
  141.8 39.4 all-gather.11
  182.8 48.3 all-gather.15
  241.8 30.1 reduce-scatter.2
  274.2 46.9 all-gather.19
  322.9 29.4 all-gather.17
  383.6 29.7 reduce-scatter.4

commit v2 on v1

--- a/solution.py
+++ b/solution.py
@@ -8,6 +8,7 @@
 from jax.sharding import PartitionSpec as P
 
 HEAD_WIDTH = 128
+LANES = 128
 
 
 epsilon = 1e-06
@@ -62,8 +63,70 @@
     return mixed.reshape(row_count, query_heads * head_size).astype(jnp.bfloat16)
 
 
-def gather_features(shard):
-    return lax.all_gather(shard, "tp", axis=1, tiled=True)
+def ring_kernel(block_ref, whole_ref, local_sem, send_sems, recv_sems):
+    ring = lax.axis_size("tp")
+    req, me = lax.axis_index("req"), lax.axis_index("tp")
+    right, left = lax.rem(me + 1, ring), lax.rem(me + ring - 1, ring)
+    rows, width = block_ref.shape
+    half = rows // 2
+
+    def columns(owner, first, count):
+        return whole_ref.at[pl.ds(first, count), pl.ds(pl.multiple_of(owner * width, width), width)]
+
+    def send(source, target, number, peer):
+        return pltpu.make_async_remote_copy(
+            src_ref=source,
+            dst_ref=target,
+            send_sem=send_sems.at[number],
+            recv_sem=recv_sems.at[number],
+            device_id=(req, peer),
+            device_id_type=pl.DeviceIdType.MESH,
+        )
+
+    barrier = pltpu.get_barrier_semaphore()
+    for peer in (left, right):
+        pl.semaphore_signal(
+            barrier, inc=1, device_id=(req, peer), device_id_type=pl.DeviceIdType.MESH
+        )
+    pl.semaphore_wait(barrier, 2)
+    mine = columns(me, 0, rows)
+    to_right = send(block_ref, mine, 0, right)
+    to_left = send(block_ref, mine, 1, left)
+    to_right.start()
+    to_left.start()
+    local = pltpu.make_async_copy(block_ref, mine, local_sem)
+    local.start()
+    to_right.wait_recv()
+    top = columns(left, 0, half)
+    on_right = send(top, top, 2, right)
+    on_right.start()
+    to_left.wait_recv()
+    bottom = columns(right, half, half)
+    on_left = send(bottom, bottom, 3, left)
+    on_left.start()
+    local.wait()
+    to_right.wait_send()
+    to_left.wait_send()
+    on_right.wait()
+    on_left.wait()
+
+
+def ring_gather(block, call_number):
+    rows, width = block.shape
+    return pl.pallas_call(
+        ring_kernel,
+        out_shape=jax.ShapeDtypeStruct((rows, width * lax.axis_size("tp")), block.dtype),
+        in_specs=[pl.BlockSpec(memory_space=pltpu.VMEM)],
+        out_specs=pl.BlockSpec(memory_space=pl.ANY),
+        scratch_shapes=[
+            pltpu.SemaphoreType.DMA,
+            pltpu.SemaphoreType.DMA((4,)),
+            pltpu.SemaphoreType.DMA((4,)),
+        ],
+        compiler_params=pltpu.CompilerParams(
+            collective_id=call_number, has_side_effects=True, vmem_limit_bytes=8 << 20
+        ),
+    )(block)
 
 
 def reduce_columns(term):
@@ -93,7 +156,7 @@
         out_shape=[jax.ShapeDtypeStruct((count, n, width), table.dtype) for n in row_counts],
         compiler_params=pltpu.CompilerParams(vmem_limit_bytes=8 << 20),
     )(index_list, table)
-    return [part.reshape(-1, width) for part in picked]
+    return picked
 
 
 def gather_owned(parts):
@@ -109,6 +172,27 @@
 
 def product(left, right):
     return jnp.dot(left, right, preferred_element_type=jnp.float32)
+
+
+def shared_low(inputs, a_rows, request, rank, call_number):
+    kinds = a_rows.shape[1] // rank
+    rows = a_rows.shape[0] * a_rows.shape[1]
+    slot = jnp.arange(rows, dtype=jnp.int32)
+    own = request[:, None] == (slot // (kinds * rank))[None, :]
+    low = low_product(inputs, a_rows.reshape(rows, -1), own)
+    lane = jnp.arange(LANES, dtype=jnp.int32)
+    fold = (slot % (kinds * rank))[:, None] == lane[None, :]
+    partial = product(low, fold.astype(jnp.bfloat16)).astype(jnp.bfloat16)
+    parts = ring_gather(partial, call_number)
+    spread_slot = jnp.arange(a_rows.shape[0] * rank, dtype=jnp.int32)
+    own_spread = request[:, None] == (spread_slot // rank)[None, :]
+    source = jnp.arange(parts.shape[1], dtype=jnp.int32) % LANES
+    lows = []
+    for kind in range(kinds):
+        expand = source[:, None] == (spread_slot % rank + kind * rank)[None, :]
+        spread = product(parts, expand.astype(jnp.bfloat16))
+        lows.append(jnp.where(own_spread, spread, 0.0).astype(jnp.bfloat16))
+    return lows
 
 
 def per_device(
@@ -144,11 +228,15 @@
     member_int, request, position, starts = request_layout(request_lens, row_count)
     pos_float = position.astype(jnp.float32)
     rank = query_adapter_output.shape[1]
-    request_count = request_lens.shape[0]
-    column_request = jnp.arange(request_count * rank, dtype=jnp.int32) // rank
-    own = request[:, None] == column_request[None, :]
-
-    whole = gather_features(tokens)
+    feature_width = tokens.shape[1]
+    first_feature = lax.axis_index("tp") * feature_width
+
+    def own_features(values):
+        return lax.dynamic_slice_in_dim(values, first_feature, feature_width, 1)
+
+    def flat(table):
+        return table.reshape(-1, table.shape[2])
+
     table_one = gather_owned(
         [
             query_key_value_adapter_input,
@@ -156,6 +244,7 @@
             jnp.concatenate([key_adapter_output, value_adapter_output], axis=2),
         ]
     )
+    whole = ring_gather(tokens, 0)
     table_two = gather_owned(
         [
             output_adapter_input,
@@ -166,62 +255,51 @@
     )
     table_three = gather_owned([gate_adapter_output, up_adapter_output, down_adapter_input])
     a_qkv, b_query, b_kv = pick_adapters(table_one, request_index_list, (3 * rank, rank, rank))
-    a_qkv = gather_features(a_qkv)
-    a_out, b_out, a_gate_up, b_down = pick_adapters(
-        table_two, request_index_list, (rank, rank, 2 * rank, rank)
-    )
-    b_gate, b_up, a_down = pick_adapters(table_three, request_index_list, (rank, rank, rank))
-    spread = gather_features(
-        jnp.concatenate([a_gate_up, b_out, b_down], axis=0)
-    )
-    pair_rows = 2 * rank * request_count
-    single_rows = rank * request_count
-    a_gate_up = spread[:pair_rows].reshape(request_count, 2, rank, -1)
-    b_out = spread[pair_rows : pair_rows + single_rows]
-    b_down = spread[pair_rows + single_rows :]
-    a_qkv = a_qkv.reshape(request_count, 3, rank, -1)
-
-    def part(stack, number):
-        return stack[:, number].reshape(single_rows, -1)
 
     normed = rms_scale(whole.astype(jnp.float32), attention_norm_gain).astype(jnp.bfloat16)
+    low_query, low_key, low_value = shared_low(own_features(normed), a_qkv, request, rank, 1)
+    b_query, b_kv = flat(b_query), flat(b_kv)
     kv_width = key_weight.shape[1]
-    query = product(normed, query_weight) + product(
-        low_product(normed, part(a_qkv, 0), own), b_query
-    )
+    query = product(normed, query_weight) + product(low_query, b_query)
     heads_here = query.shape[1] // HEAD_WIDTH
     query = rotate(
         rms_scale(query.reshape(row_count, heads_here, HEAD_WIDTH), query_norm_gain), pos_float
     ).astype(jnp.bfloat16)
-    keys = product(normed, key_weight) + product(
-        low_product(normed, part(a_qkv, 1), own), b_kv[:, :kv_width]
-    )
+    keys = product(normed, key_weight) + product(low_key, b_kv[:, :kv_width])
     kv_here = keys.shape[1] // HEAD_WIDTH
     keys = rotate(
         rms_scale(keys.reshape(row_count, kv_here, HEAD_WIDTH), key_norm_gain), pos_float
     ).astype(jnp.bfloat16)
-    values = (
-        product(normed, value_weight)
-        + product(low_product(normed, part(a_qkv, 2), own), b_kv[:, kv_width:])
+    values = (product(normed, value_weight) + product(low_value, b_kv[:, kv_width:])).astype(
+        jnp.bfloat16
+    )
+    attended = attend(query, keys, values.reshape(row_count, kv_here, HEAD_WIDTH), request)
+    share = product(attended, output_weight).astype(jnp.bfloat16)
+    share, table_two, table_three = lax.optimization_barrier((share, table_two, table_three))
+    summed = reduce_columns(share)
+    a_out, b_out, a_gate_up, b_down = pick_adapters(
+        table_two, request_index_list, (rank, rank, 2 * rank, rank)
+    )
+    b_gate, b_up, a_down = pick_adapters(table_three, request_index_list, (rank, rank, rank))
+    (low_out,) = shared_low(attended, a_out, request, rank, 2)
+    resid = (
+        summed.astype(jnp.float32) + product(low_out, flat(b_out)) + tokens.astype(jnp.float32)
     ).astype(jnp.bfloat16)
-    attended = attend(query, keys, values.reshape(row_count, kv_here, HEAD_WIDTH), request)
-    share = product(attended, output_weight) + product(low_product(attended, a_out, own), b_out)
-    summed = reduce_columns(share.astype(jnp.bfloat16))
-    resid = (summed.astype(jnp.float32) + tokens.astype(jnp.float32)).astype(jnp.bfloat16)
-    whole_two = gather_features(resid)
+    whole_two = ring_gather(resid, 3)
     normed_two = rms_scale(whole_two.astype(jnp.float32), feedforward_norm_gain).astype(
         jnp.bfloat16
     )
-    gate = product(normed_two, gate_weight) + product(
-        low_product(normed_two, part(a_gate_up, 0), own), b_gate
-    )
-    upward = product(normed_two, up_weight) + product(
-        low_product(normed_two, part(a_gate_up, 1), own), b_up
-    )
+    low_gate, low_up = shared_low(own_features(normed_two), a_gate_up, request, rank, 4)
+    gate = product(normed_two, gate_weight) + product(low_gate, flat(b_gate))
+    upward = product(normed_two, up_weight) + product(low_up, flat(b_up))
     hidden = (jax.nn.silu(gate) * upward).astype(jnp.bfloat16)
-    share_two = product(hidden, down_weight) + product(low_product(hidden, a_down, own), b_down)
-    summed_two = reduce_columns(share_two.astype(jnp.bfloat16))
-    return (summed_two.astype(jnp.float32) + resid.astype(jnp.float32)).astype(jnp.bfloat16)
+    summed_two = reduce_columns(product(hidden, down_weight).astype(jnp.bfloat16))
+    (low_down,) = shared_low(hidden, a_down, request, rank, 5)
+    return (
+        summed_two.astype(jnp.float32)
+        + product(low_down, flat(b_down))
+        + resid.astype(jnp.float32)
+    ).astype(jnp.bfloat16)
 
 
 def solution(mesh):

time: 423 us -> 294 us (0.70)
  waiting for transfers between devices: 290 us -> 85.3 us
  Pallas kernels: 2.63 us -> 83.7 us
  matrix products: 64.4 us -> 56.2 us
  local copies, waits for them, and re-layouts: 28.5 us -> 33.1 us
    all_gather x4 -> x0, waiting for transfers between devices: 95 us -> none  [gather_features(): return lax.all_gather(shard, 'tp', axis=1, tiled=True)]
    pallas_call x0 -> x6, Pallas kernels: none -> 80.7 us  [ring_gather(): pl.pallas_call(ring_kernel, out_shape=jax.ShapeDtypeStruct((rows, width *...]
    all_gather x3, waiting for transfers between devices: 136 us -> 57.1 us  [gather_owned(): lax.all_gather(jnp.concatenate(parts, axis=1), 'req', axis=0, tiled=True)]
    reduce_scatter x2, waiting for transfers between devices: 58.7 us -> 28.1 us  [reduce_columns(): return lax.psum_scatter(term, 'tp', scatter_dimension=1, tiled=True)]
    unnamed x62 -> x90, local copies, waits for them, and re-layouts: 14 us -> 22.8 us
    dot_general x14 -> x18, matrix products: 60.7 us -> 53.3 us  [product(): return jnp.dot(left, right, preferred_element_type=jnp.float32)]
    slice x4 -> x0, local copies, waits for them, and re-layouts: 6.67 us -> none  [the longest x2 5.08 us: part(): return stack[:, number].reshape(single_rows, -1)]
  transfers between devices with their start and end apart: 9 -> 5, of which waited for: 9 -> 4; matrix products, arithmetic and copies ran while one was open for 13% -> 19% of each run, Pallas kernels for 1% -> 19%
where the time goes in v2:
time: 294 us; the launch traced here: 293 us
  waiting for transfers between devices  85.3 us (29%)
  Pallas kernels  83.7 us (28%)
  matrix products  56.2 us (19%)
  local copies, waits for them, and re-layouts  33.1 us (11%)
  other arithmetic  20.6 us (7%)
  between operations  13.6 us (5%)
    pallas_call x6, Pallas kernels, ring_gather(): pl.pallas_call(ring_kernel, out_shape=jax.ShapeDtypeStruct((rows, width *...  80.7 us
    all_gather x3, waiting for transfers between devices, gather_owned(): lax.all_gather(jnp.concatenate(parts, axis=1), 'req', axis=0, tiled=True)  57.1 us
    dot_general x18, matrix products, product(): return jnp.dot(left, right, preferred_element_type=jnp.float32)  53.3 us
    reduce_scatter x2, waiting for transfers between devices, reduce_columns(): return lax.psum_scatter(term, 'tp', scatter_dimension=1, tiled=True)  28.1 us
    unnamed x90, local copies, waits for them, and re-layouts  22.8 us
  transfers between devices with their start and end apart: 5, of which 4 were waited for; matrix products, arithmetic and copies ran while one was open for 19% of the time, Pallas kernels for 19%

profile of v2, /device:TPU:1, one launch (start us, length us, event | category | flops | bytes accessed | tf_op | source)
XLA Modules:
  0.0 292.7 jit_solution(3398839852411074460)
XLA Ops:
  13.6 21.5 %shard_map.235 = bf16[512,2048]{1,0:T(8,128)(2,1)S(1)} custom-call(bf16[512,512]{1,0:T(8,128)(2,1)S(1)} %copy-done.8), custom_call_target="tpu_custom_call" | custom-call | tf_op jit(solution)/shard_map/pallas_call | solution.py:116
  43.9 2.1 fusion
  47.9 2.3 fusion.169
  50.3 10.3 %all-gather.4.cloned.1.call-done.table_ref = bf16[64,80,512]{2,1,0:T(8,128)(2,1)} async-done(((bf16[2,80,512]{2,1,0:T(8,128)(2,1)}), bf16[64,80,512]{2,1,0:T(8,128)(2,1)}) %all-gather.4.cloned.1.call-update) | async-done | bytes 5242896 | tf_op jit(solution)/shard_map/all_gather | solution.py:163
  60.6 2.5 copy-done.4
  65.8 2.2 fusion.34.block_ref
  68.0 9.0 %shard_map.237 = bf16[512,512]{1,0:T(8,128)(2,1)S(1)} custom-call(bf16[512,128]{1,0:T(8,128)(2,1)S(1)} %fusion.34.block_ref), custom_call_target="tpu_custom_call" | custom-call | tf_op jit(solution)/shard_map/pallas_call | solution.py:116
  77.8 3.3 %multiply_reduce_fusion = (f32[512,4]{0,1:T(4,128)S(1)}, f32[512,512]{0,1:T(8,128)}) fusion(f32[512,512]{0,1:T(8,128)} %fusion.169, bf16[256,512]{1,0:T(8,128)(2,1)S(1)} %bitcast.83, bf16[512,512]{1,0:T(8,128)(2,1)} %copy-done.6, s32[256]{0:T(256)} %and_select_fusion, s32[256]{0:T(256)} %get-tuple-element.47, s32[512]{0:T(512)S(1)} %get-tuple-element.32, ...), kind=kOutput, calls=%fused_computation.61 | convolution fusion | flops 269744128 | bytes 2897920 | tf_op jit(solution)/shard_map/dot_general | solution.py:174
  87.5 2.5 fusion.28
  89.9 3.6 %multiply_reduce_fusion.1 = (f32[512,2]{0,1:T(2,128)S(1)}, f32[512,256]{0,1:T(8,128)}) fusion(f32[512,256]{0,1:T(8,128)} %fusion.28, bf16[512,2048]{1,0:T(8,128)(2,1)} %copy-done.23, bf16[2048,256]{1,0:T(8,128)(2,1)} %param.33), kind=kOutput, calls=%fused_computation.86 | convolution fusion | flops 537263104 | bytes 4198400 | tf_op jit(solution)/shard_map/dot_general | solution.py:174
  93.5 2.0 copy.58
  95.6 2.0 multiply_multiply_fusion.1
  97.6 2.5 fusion.29
  102.3 2.3 fusion.16
  108.3 2.6 convolution_convert_fusion.1
  110.9 46.8 %all-gather.6.cloned.1.call-done.table_ref = bf16[64,80,512]{2,1,0:T(8,128)(2,1)} async-done(((bf16[2,80,512]{2,1,0:T(8,128)(2,1)}), bf16[64,80,512]{2,1,0:T(8,128)(2,1)}) %all-gather.6.cloned.1.call-update) | async-done | bytes 5242896 | tf_op jit(solution)/shard_map/all_gather | solution.py:163
  158.4 2.5 copy-done.3
  165.7 14.6 %shard_map.239 = bf16[512,512]{1,0:T(8,128)(2,1)S(1)} custom-call(bf16[512,128]{1,0:T(8,128)(2,1)S(1)} %fusion.31.block_ref), custom_call_target="tpu_custom_call" | custom-call | tf_op jit(solution)/shard_map/pallas_call | solution.py:116
  181.2 2.4 copy-done.5
  186.0 6.2 %reduce-scatter.3.cloned.1.call-done = bf16[512,512]{1,0:T(8,128)(2,1)} async-done(((bf16[512,2048]{1,0:T(8,128)(2,1)}), bf16[512,512]{1,0:T(8,128)(2,1)}) %reduce-scatter.3.cloned.1.call-update) | async-done | bytes 524304 | tf_op jit(solution)/shard_map/reduce_scatter | solution.py:133
  192.2 3.0 %fusion.11.block_ref = bf16[512,512]{1,0:T(8,128)(2,1)} fusion(bf16[256,512]{1,0:T(8,128)(2,1)} %bitcast.94, bf16[512,512]{1,0:T(8,128)(2,1)} %copy-done.11, bf16[512,512]{1,0:T(8,128)(2,1)} %block_ref.1, bf16[512,512]{1,0:T(8,128)(2,1)} %reduce-scatter.3.cloned.1.call-done, s32[256]{0:T(256)} %and_select_fusion, s32[256]{0:T(256)S(1)} %copy-done.34, ...), kind=kOutput, calls=%fused_computation.34 | convolution fusion | flops 270270464 | bytes 2365440 | tf_op jit(solution)/shard_map/dot_general | solution.py:174
  196.3 19.4 %shard_map.240 = bf16[512,2048]{1,0:T(8,128)(2,1)S(1)} custom-call(bf16[512,512]{1,0:T(8,128)(2,1)S(1)} %copy-done.9), custom_call_target="tpu_custom_call" | custom-call | tf_op jit(solution)/shard_map/pallas_call | solution.py:116
  218.1 2.6 fusion.33.block_ref
  221.6 8.4 %shard_map.241 = bf16[512,512]{1,0:T(8,128)(2,1)S(1)} custom-call(bf16[512,128]{1,0:T(8,128)(2,1)S(1)} %copy-done.12), custom_call_target="tpu_custom_call" | custom-call | tf_op jit(solution)/shard_map/pallas_call | solution.py:116
  230.8 5.6 %fusion.170 = f32[512,768]{1,0:T(8,128)} fusion(bf16[512,2048]{1,0:T(8,128)(2,1)} %fusion.5, bf16[2048,768]{1,0:T(8,128)(2,1)} %param.36), kind=kOutput, calls=%fused_computation.214 | convolution fusion | flops 1610612736 | bytes 6815744 | tf_op jit(solution)/shard_map/dot_general | solution.py:174
  236.4 3.0 %fusion.171 = f32[512,768]{1,0:T(8,128)} fusion(bf16[512,2048]{1,0:T(8,128)(2,1)S(1)} %copy-done.25, bf16[2048,768]{1,0:T(8,128)(2,1)S(1)} %copy-done.41), kind=kOutput, calls=%fused_computation.215 | convolution fusion | flops 1610612736 | bytes 6815744 | tf_op jit(solution)/shard_map/dot_general | solution.py:174
  239.4 2.9 fusion.30
  242.3 4.4 %multiply_convert_fusion = bf16[512,768]{1,0:T(8,128)(2,1)} fusion(f32[512,768]{1,0:T(8,128)} %fusion.171, f32[512,768]{1,0:T(8,128)} %fusion.170, f32[512,768]{1,0:T(8,128)} %fusion.30, bf16[256,768]{1,0:T(8,128)(2,1)} %bitcast.90, bf16[512,512]{1,0:T(8,128)(2,1)} %copy-done.7, s32[256]{0:T(256)} %broadcast_add_fusion.1, s32[256]{0:T(256)S(1)} %copy-done.34, ...), kind=kOutput, calls=%fused_computation.25 | convolution fusion | flops 339214336 | bytes 6428672 | tf_op jit(solution)/shard_map/dot_general | solution.py:174
  246.6 4.3 %convolution_convert_fusion = bf16[512,2048]{1,0:T(8,128)(2,1)} fusion(bf16[512,768]{1,0:T(8,128)(2,1)} %multiply_convert_fusion, bf16[768,2048]{1,0:T(8,128)(2,1)S(1)} %copy-done), kind=kOutput, calls=%fused_computation.13 | convolution fusion | flops 1611661312 | bytes 6029312 | tf_op jit(solution)/shard_map/dot_general | solution.py:174
  252.8 7.7 %shard_map.243 = bf16[512,512]{1,0:T(8,128)(2,1)S(1)} custom-call(bf16[512,128]{1,0:T(8,128)(2,1)S(1)} %fusion.32.block_ref), custom_call_target="tpu_custom_call" | custom-call | tf_op jit(solution)/shard_map/pallas_call | solution.py:116
  261.3 21.9 %reduce-scatter.5.cloned.1.call-done = bf16[512,512]{1,0:T(8,128)(2,1)} async-done(((bf16[512,2048]{1,0:T(8,128)(2,1)}), bf16[512,512]{1,0:T(8,128)(2,1)}) %reduce-scatter.5.cloned.1.call-update) | async-done | bytes 524304 | tf_op jit(solution)/shard_map/reduce_scatter | solution.py:133
  283.2 2.9 fusion.12
  (138 shorter events, 49.8 us)
Async XLA Ops:
  6.5 240.1 %copy-start = (bf16[768,2048]{1,0:T(8,128)(2,1)S(1)}, bf16[768,2048]{1,0:T(8,128)(2,1)}, u32[]{:S(2)}) copy-start(bf16[768,2048]{1,0:T(8,128)(2,1)} %param.38) | copy-start | bytes 9437188
  6.5 29.9 %copy-start.40 = (s32[1,16]{1,0:T(1,128)S(1)}, s32[1,16]{1,0:T(1,128)}, u32[]{:S(2)}) copy-start(s32[1,16]{1,0:T(1,128)} %param.26) | copy-start | bytes 196
  6.5 54.1 %all-gather.4.cloned.1.call-start = ((), (), s32[]{:S(2)}) async-start(), calls=%async_computation.2 | async-start | bytes 5406720 | tf_op jit(solution)/shard_map/all_gather | solution.py:163
  8.4 102.6 %all-gather.8.cloned.1.call-start = ((), (), s32[]{:S(2)}) async-start(), calls=%async_computation.4 | async-start | bytes 4866048 | tf_op jit(solution)/shard_map/all_gather | solution.py:163
  10.0 147.8 %all-gather.6.cloned.1.call-start = ((), (), s32[]{:S(2)}) async-start(), calls=%async_computation.3 | async-start | bytes 5406720 | tf_op jit(solution)/shard_map/all_gather | solution.py:163
  11.6 180.6 %reduce-scatter.3.cloned.1.call-start = ((), (), s32[]{:S(2)}) async-start(), calls=%async_computation.5 | async-start | bytes 2621440 | tf_op jit(solution)/shard_map/reduce_scatter | solution.py:133
  36.4 9.6 %copy-start.35 = (f32[2048]{0:T(1024)S(1)}, f32[2048]{0:T(1024)}, u32[]{:S(2)}) copy-start(f32[2048]{0:T(1024)} %param.28) | copy-start | bytes 24580
  37.1 9.5 %copy-start.26 = (f32[512,64]{0,1:T(8,128)}, f32[512,64]{0,1:T(8,128)S(1)}, u32[]{:S(2)}) copy-start(f32[512,64]{0,1:T(8,128)S(1)} %get-tuple-element.37) | copy-start | bytes 393220
  37.1 9.5 %copy-start.28 = (f32[512,64]{0,1:T(8,128)}, f32[512,64]{0,1:T(8,128)S(1)}, u32[]{:S(2)}) copy-start(f32[512,64]{0,1:T(8,128)S(1)} %get-tuple-element.38) | copy-start | bytes 393220
  41.7 4.3 %copy-start.2 = (bf16[512,2048]{1,0:T(8,128)(2,1)S(1)}, bf16[512,2048]{1,0:T(8,128)(2,1)}, u32[]{:S(2)}) copy-start(bf16[512,2048]{1,0:T(8,128)(2,1)} %copy-done.1) | copy-start | bytes 6291460
  46.0 1.9 copy-start.42
  47.9 12.7 %copy-start.13 = (s32[1,16]{1,0:T(1,128)S(1)}, s32[1,16]{1,0:T(1,128)}, u32[]{:S(2)}) copy-start(s32[1,16]{1,0:T(1,128)} %param.27) | copy-start | bytes 196
  60.6 2.5 copy-start.4
  77.8 4.7 %copy-start.27 = (f32[512,64]{0,1:T(8,128)S(1)}, f32[512,64]{0,1:T(8,128)}, u32[]{:S(2)}) copy-start(f32[512,64]{0,1:T(8,128)} %copy-done.26) | copy-start | bytes 393220
  82.5 4.9 %copy-start.21 = (bf16[16,16,512]{2,1,0:T(8,128)(2,1)S(1)}, bf16[16,16,512]{2,1,0:T(8,128)(2,1)}, u32[]{:S(2)}) copy-start(bf16[16,16,512]{2,1,0:T(8,128)(2,1)} %copy-done.20) | copy-start | bytes 786436
  82.5 4.9 %copy-start.33 = (s32[512]{0:T(512)S(1)}, s32[512]{0:T(512)}, u32[]{:S(2)}) copy-start(s32[512]{0:T(512)} %add_select_fusion.2) | copy-start | bytes 6148
  82.6 4.9 %copy-start.34 = (s32[256]{0:T(256)S(1)}, s32[256]{0:T(256)}, u32[]{:S(2)}) copy-start(s32[256]{0:T(256)} %get-tuple-element.47) | copy-start | bytes 3076
  89.9 5.7 %copy-start.39 = (f32[128]{0:T(128)S(1)}, f32[128]{0:T(128)}, u32[]{:S(2)}) copy-start(f32[128]{0:T(128)} %param.30) | copy-start | bytes 1540
  93.5 4.1 %copy-start.38 = (s32[256]{0:T(256)S(1)}, s32[256]{0:T(256)}, u32[]{:S(2)}) copy-start(s32[256]{0:T(256)} %get-tuple-element.48) | copy-start | bytes 3076
  100.1 2.2 copy-start.24
  102.3 2.3 copy-start.30
  102.3 2.3 copy-start.31
  102.3 2.3 copy-start.32
  106.2 2.1 copy-start.43
  157.7 125.5 %reduce-scatter.5.cloned.1.call-start = ((), (), s32[]{:S(2)}) async-start(), calls=%async_computation.6 | async-start | bytes 2621440 | tf_op jit(solution)/shard_map/reduce_scatter | solution.py:133
  158.4 2.5 copy-start.3
  181.2 2.4 copy-start.5
  196.3 19.9 %copy-start.36 = (f32[2048]{0:T(1024)S(1)}, f32[2048]{0:T(1024)}, u32[]{:S(2)}) copy-start(f32[2048]{0:T(1024)} %param.31) | copy-start | bytes 24580
  230.8 5.6 %copy-start.25 = (bf16[512,2048]{1,0:T(8,128)(2,1)S(1)}, bf16[512,2048]{1,0:T(8,128)(2,1)}, u32[]{:S(2)}) copy-start(bf16[512,2048]{1,0:T(8,128)(2,1)} %fusion.5) | copy-start | bytes 6291460
  230.8 5.6 %copy-start.41 = (bf16[2048,768]{1,0:T(8,128)(2,1)S(1)}, bf16[2048,768]{1,0:T(8,128)(2,1)}, u32[]{:S(2)}) copy-start(bf16[2048,768]{1,0:T(8,128)(2,1)} %param.37) | copy-start | bytes 9437188
  236.4 3.0 %copy-start.37 = (s32[256]{0:T(256)S(1)}, s32[256]{0:T(256)}, u32[]{:S(2)}) copy-start(s32[256]{0:T(256)} %and_select_fusion) | copy-start | bytes 3076
  250.9 32.3 %copy-start.19 = (bf16[16,16,512]{2,1,0:T(8,128)(2,1)S(1)}, bf16[16,16,512]{2,1,0:T(8,128)(2,1)}, u32[]{:S(2)}) copy-start(bf16[16,16,512]{2,1,0:T(8,128)(2,1)} %copy-done.18) | copy-start | bytes 786436
  (18 other events, 16.4 us)
Sparse Core Ops, SparseCore 0:
  9.6 50.9 all-gather.3
  62.9 45.8 all-gather.7
  111.0 46.6 all-gather.5
  160.0 32.1 reduce-scatter.2
  251.1 32.1 reduce-scatter.4
